TPU v7x, 32 devices: a whole 2x2x4 slice. The times are simulated.
32 devices in a mesh: col: 4 (over z), row: 8 (over y, x, core).
Axes of the slice: x: 2, y: 2, z: 4, core: 2. Of those that a mesh axis runs over, the one named last changes fastest.
Arguments:
- affinity: bfloat16 [3840, 128, 128], P(('col', 'row')), may hold values from 0 to 0.015625
- tile_rows: int32 [3840], P(('col', 'row')), may hold values from 0 to 19
- tile_cols: int32 [3840], P(('col', 'row')), may hold values from 0 to 39
- live_tiles: int32 [32], P(('col', 'row')), may hold values from 1 to 120, as said below
- start: float32 [20480, 256], P(('col', 'row')), may hold values from -1500 to 1500
Outputs:
- vectors: float32 [20480, 256], P(('col', 'row'))
- first_passes: float32 [2, 20480, 256], P(None, ('col', 'row'))
Inputs may be any that keep to these rules, and one draw needn't show every extreme that they name: A device's tiles are its slots 0 to live_tiles - 1; later slots are ignored. Some device holds exactly 120 tiles.
All inputs are finite; a program needn't handle non-finite values.
Results may differ from a plain program's by a relative error of at most 0.0003.
Values sent between devices are 32-bit elements; how exact they have to be, the bound alone decides.
No kernel may reach another device: no remote copies, remote signals or barrier semaphores. Data moves between devices by JAX's collectives and lax.ppermute only.
A program may use at most 128 MiB of HBM per device.

v0:
```python
import jax
import jax.numpy as jnp
from jax import lax
from jax.sharding import PartitionSpec as P

ITERS = 2
highest = lax.Precision.HIGHEST


def local_gram(matrix):
    return jnp.dot(matrix.T, matrix, precision=highest, preferred_element_type=jnp.float32)


def inverse_lower(gram):
    lower = jnp.linalg.cholesky(gram)
    return jax.scipy.linalg.solve_triangular(
        lower, jnp.eye(gram.shape[0], dtype=jnp.float32), lower=True
    )


def apply_factor(matrix, inverse):
    return jnp.dot(matrix, inverse.T, precision=highest, preferred_element_type=jnp.float32)


def body(affinity, tile_rows, tile_cols, live_tiles, start):
    n_row = lax.axis_size("row")
    n_col = lax.axis_size("col")
    slot_count = affinity.shape[0]
    tile_size = affinity.shape[1]
    rows_local = start.shape[0]
    vec_count = start.shape[1]
    own_tiles = rows_local // tile_size
    live = (jnp.arange(slot_count) < live_tiles[0]).astype(jnp.float32)
    row_onehot = (jnp.arange(own_tiles * n_col)[:, None] == tile_rows[None, :]).astype(
        jnp.float32
    ) * live[None, :]
    row_sums = jnp.sum(affinity, axis=2, dtype=jnp.float32)
    degree_terms = jnp.dot(
        row_onehot, row_sums, precision=highest, preferred_element_type=jnp.float32
    )
    degree = 1.0 + lax.psum_scatter(degree_terms, "col", scatter_dimension=0, tiled=True).reshape(
        rows_local
    )
    scaling = (1.0 / jnp.sqrt(degree))[:, None]
    squares = affinity.astype(jnp.float32)
    firsts = []
    pending = start
    for step_number in range(ITERS):
        mapped_scaled = scaling * pending
        gathered = lax.all_gather(mapped_scaled, "row", axis=0, tiled=True)
        gathered = gathered.reshape(n_row * own_tiles, tile_size, vec_count)
        picked = gathered[tile_cols]
        products = jnp.einsum(
            "sij,sjk->sik", squares, picked, precision=highest, preferred_element_type=jnp.float32
        )
        terms = jnp.dot(
            row_onehot,
            products.reshape(slot_count, tile_size * vec_count),
            precision=highest,
            preferred_element_type=jnp.float32,
        )
        summed = lax.psum_scatter(terms, "col", scatter_dimension=0, tiled=True)
        raw_image = scaling * (mapped_scaled + summed.reshape(rows_local, vec_count))
        if step_number == 0:
            inner_gram = lax.psum(local_gram(raw_image), ("col", "row"))
            image_block = raw_image
        else:
            raw_gram, pending_gram = lax.psum(
                (local_gram(raw_image), local_gram(pending)), ("col", "row")
            )
            pending_inverse = inverse_lower(pending_gram)
            image_block = apply_factor(raw_image, pending_inverse)
            inner_gram = jnp.dot(
                jnp.dot(
                    pending_inverse, raw_gram, precision=highest, preferred_element_type=jnp.float32
                ),
                pending_inverse.T,
                precision=highest,
                preferred_element_type=jnp.float32,
            )
        pending = apply_factor(image_block, inverse_lower(inner_gram))
        firsts.append(pending)
    final_gram = lax.psum(local_gram(pending), ("col", "row"))
    basis = apply_factor(pending, inverse_lower(final_gram))
    total_images = rows_local * n_row * n_col
    root = jnp.sqrt(jnp.float32(total_images))
    return (root * basis, root * jnp.stack(firsts, axis=0))


def solution(mesh):
    placed = (
        P(("col", "row"), None, None),
        P(("col", "row")),
        P(("col", "row")),
        P(("col", "row")),
        P(("col", "row"), None),
    )
    return jax.shard_map(
        body,
        mesh=mesh,
        in_specs=placed,
        out_specs=(P(("col", "row"), None), P(None, ("col", "row"), None)),
        check_vma=False,
    )
```

profile of v0, /device:TPU:0, one launch (start us, length us, event | category | flops | bytes accessed | tf_op | source)
XLA Modules:
  0.0 1157.0 jit_solution(773065271221598994)
XLA Ops:
  7.9 3.2 convert_reduce_fusion
  11.9 20.4 %all-reduce.1 = f32[20,128]{1,0:T(8,128)S(1)} all-reduce(f32[20,128]{1,0:T(8,128)S(1)} %fusion.55), channel_id=2, replica_groups=mesh['col'=4,'row'=8] {'col'}, use_global_device_ids=true, to_apply=%region_1.0.clone | all-reduce | flops 2560 | bytes 20480
  34.4 2.1 broadcast_multiply_fusion.1
  36.6 39.3 %all-gather.3.cloned.1.call-done = f32[5120,256]{1,0:T(8,128)} async-done(((f32[640,256]{1,0:T(8,128)}), f32[5120,256]{1,0:T(8,128)}) %all-gather.3.cloned.1.call-update) | async-done | bytes 5242896 | tf_op jit(solution)/shard_map/all_gather | solution.py:50
  75.9 12.1 %gather_fusion = f32[120,128,256]{2,1,0:T(8,128)} fusion(f32[40,128,256]{2,1,0:T(8,128)} %bitcast.166, s32[1024]{0:T(1024)S(1)} %pad_clamp_fusion), kind=kCustom, calls=%fused_computation | custom fusion | bytes 31457760 | tf_op jit(solution)/shard_map/gather | solution.py:52
  88.0 20.2 %convolution_bitcast_fusion.1 = f32[120,128,256]{1,2,0:T(8,128)} fusion(f32[120,128,256]{2,1,0:T(8,128)} %gather_fusion, bf16[120,128,128]{2,1,0:T(8,128)(2,1)} %param.8), kind=kOutput, calls=%fused_computation.11 | convolution fusion | flops 6039797760 | bytes 35389440 | tf_op jit(solution)/shard_map/sij,sjk->sik/dot_general | solution.py:53
  108.2 15.7 %copy.41 = f32[15,8,128,256]{3,1,2,0:T(8,128)} copy(f32[15,8,128,256]{2,3,1,0:T(8,128)} %bitcast.163) | data formatting | bytes 31457280
  123.9 10.5 fusion.53
  134.4 78.5 %fusion = f32[8,32768]{1,0:T(8,128)} fusion(f32[20,32768]{1,0:T(8,128)S(1)} %fusion.53), kind=kCustom, calls=%all-reduce-scatter | all-reduce-scatter fusion | flops 1048577 | bytes 3670528
  215.7 2.6 collective-permute-start.1
  219.0 20.1 %collective-permute-done.1 = f32[1,32768]{1,0:T(1,128)S(1)} collective-permute-done((f32[1,32768]{1,0:T(1,128)S(1)}, f32[1,32768]{1,0:T(1,128)S(1)}, u32[]{:S(2)}, u32[]{:S(2)}) %collective-permute-start.1) | collective-permute-done | bytes 131104
  239.1 21.2 %concatenate.3 = f32[17,32768]{1,0:T(8,128)} concatenate(f32[1,32768]{1,0:T(1,128)S(1)} %collective-permute-done.1, f32[8,32768]{1,0:T(8,128)S(1)} %collective-permute-done, f32[8,32768]{1,0:T(8,128)} %fusion), dimensions={0} | concatenate | bytes 4456448
  262.4 2.2 fusion.29
  264.6 129.0 %all-reduce.11.cloned.1.call-done = f32[256,256]{0,1:T(8,128)} async-done(((f32[256,256]{0,1:T(8,128)}), f32[256,256]{0,1:T(8,128)}) %all-reduce.11.cloned.1.call-update) | async-done | bytes 262160 | tf_op jit(solution)/shard_map/psum | solution.py:65
  395.7 11.7 %cholesky.214 = f32[128,128]{1,0:T(8,128)S(1)} custom-call(f32[128,128]{1,0:T(8,128)S(1)} %cholesky.346), custom_call_target="Cholesky" | custom-call | tf_op jit(solution)/shard_map/jit(cholesky)/cholesky | solution.py:15
  407.5 9.8 custom-call.17
  417.8 11.7 %cholesky.231 = f32[128,128]{1,0:T(8,128)S(1)} custom-call(f32[128,128]{1,0:T(8,128)S(1)} %convolution_subtract_fusion.7), custom_call_target="Cholesky" | custom-call | tf_op jit(solution)/shard_map/jit(cholesky)/cholesky | solution.py:15
  431.8 15.1 %while.8 = (s32[]{:T(128)}, f32[256,256]{1,0:T(8,128)S(1)}, s32[2,2]{1,0:T(2,128)S(1)}, f32[2,128,128]{2,1,0:T(8,128)S(1)}, s32[]{:T(128)}) while((s32[]{:T(128)}, f32[256,256]{1,0:T(8,128)S(1)}, s32[2,2]{1,0:T(2,128)S(1)}, f32[2,128,128]{2,1,0:T(8,128)S(1)}, s32[]{:T(128)}) %tuple.83), condition=%wide.while_cond, body=%wide.while_body.sunk | while | flops 2 | bytes 131181 | solution.py:16
  446.9 19.7 %custom-call.18 = f32[2,128,128]{1,2,0:T(8,128)S(1)} custom-call(f32[2,128,128]{2,1,0:T(8,128)S(1)} %get-tuple-element.30), custom_call_target="InvertDiagBlocksLowerTriangular" | custom-call | tf_op jit(solution)/shard_map/jit(_solve_triangular)/triangular_solve | solution.py:16
  469.1 40.2 %all-gather.5.cloned.1.call-done = f32[5120,256]{1,0:T(8,128)} async-done(((f32[640,256]{1,0:T(8,128)}), f32[5120,256]{1,0:T(8,128)}) %all-gather.5.cloned.1.call-update) | async-done | bytes 5242896 | tf_op jit(solution)/shard_map/all_gather | solution.py:50
  509.3 12.1 %gather_fusion.1 = f32[120,128,256]{2,1,0:T(8,128)} fusion(f32[40,128,256]{2,1,0:T(8,128)} %bitcast.167, s32[1024]{0:T(1024)S(1)} %pad_clamp_fusion), kind=kCustom, calls=%fused_computation.1 | custom fusion | bytes 31457760 | tf_op jit(solution)/shard_map/gather | solution.py:52
  521.4 20.2 %convolution_bitcast_fusion = f32[120,128,256]{1,2,0:T(8,128)} fusion(f32[120,128,256]{2,1,0:T(8,128)} %gather_fusion.1, bf16[120,128,128]{2,1,0:T(8,128)(2,1)} %param.8), kind=kOutput, calls=%fused_computation.10 | convolution fusion | flops 6039797760 | bytes 35389440 | tf_op jit(solution)/shard_map/sij,sjk->sik/dot_general | solution.py:53
  541.6 15.7 %copy.42 = f32[15,8,128,256]{3,1,2,0:T(8,128)} copy(f32[15,8,128,256]{2,3,1,0:T(8,128)} %bitcast.165) | data formatting | bytes 31457280
  557.3 11.6 fusion.51
  568.9 78.6 %fusion.1 = f32[8,32768]{1,0:T(8,128)S(1)} fusion(f32[20,32768]{1,0:T(8,128)} %fusion.51), kind=kCustom, calls=%all-reduce-scatter.1 | all-reduce-scatter fusion | flops 1048577 | bytes 3670528
  647.4 2.3 collective-permute-start.2
  651.5 1.9 fusion.82
  653.4 19.9 %collective-permute-done.3 = f32[1,32768]{1,0:T(1,128)S(1)} collective-permute-done((f32[1,32768]{1,0:T(1,128)S(1)}, f32[1,32768]{1,0:T(1,128)S(1)}, u32[]{:S(2)}, u32[]{:S(2)}) %collective-permute-start.3) | collective-permute-done | bytes 131104
  673.3 21.2 %concatenate.4 = f32[17,32768]{1,0:T(8,128)} concatenate(f32[1,32768]{1,0:T(1,128)S(1)} %collective-permute-done.3, f32[8,32768]{1,0:T(8,128)} %collective-permute-done.2, f32[8,32768]{1,0:T(8,128)S(1)} %fusion.1), dimensions={0} | concatenate | bytes 4456448
  696.6 2.1 fusion.30
  698.8 131.3 %all-reduce.15.cloned.1.call-done = (f32[256,256]{0,1:T(8,128)}, f32[256,256]{1,0:T(8,128)}) async-done(((f32[256,256]{0,1:T(8,128)}, f32[256,256]{1,0:T(8,128)}), (f32[256,256]{0,1:T(8,128)}, f32[256,256]{1,0:T(8,128)})) %all-reduce.15.cloned.1.call-update) | async-done | bytes 524304 | tf_op jit(solution)/shard_map/psum | solution.py:68
  832.2 11.7 %cholesky.248 = f32[128,128]{1,0:T(8,128)S(1)} custom-call(f32[128,128]{1,0:T(8,128)S(1)} %cholesky.349), custom_call_target="Cholesky" | custom-call | tf_op jit(solution)/shard_map/jit(cholesky)/cholesky | solution.py:15
  844.0 9.8 custom-call.19
  854.3 11.7 %cholesky.265 = f32[128,128]{1,0:T(8,128)S(1)} custom-call(f32[128,128]{1,0:T(8,128)S(1)} %convolution_subtract_fusion.6), custom_call_target="Cholesky" | custom-call | tf_op jit(solution)/shard_map/jit(cholesky)/cholesky | solution.py:15
  868.7 4.0 while.9
  872.7 19.8 %custom-call.20 = f32[2,128,128]{1,2,0:T(8,128)S(1)} custom-call(f32[2,128,128]{2,1,0:T(8,128)S(1)} %get-tuple-element.31), custom_call_target="InvertDiagBlocksLowerTriangular" | custom-call | tf_op jit(solution)/shard_map/jit(_solve_triangular)/triangular_solve | solution.py:16
  895.2 11.7 %cholesky.282 = f32[128,128]{1,0:T(8,128)S(1)} custom-call(f32[128,128]{1,0:T(8,128)S(1)} %cholesky.352), custom_call_target="Cholesky" | custom-call | tf_op jit(solution)/shard_map/jit(cholesky)/cholesky | solution.py:15
  907.0 9.8 custom-call.21
  917.3 11.9 %cholesky.299 = f32[128,128]{1,0:T(8,128)S(1)} custom-call(f32[128,128]{1,0:T(8,128)S(1)} %convolution_subtract_fusion.5), custom_call_target="Cholesky" | custom-call | tf_op jit(solution)/shard_map/jit(cholesky)/cholesky | solution.py:15
  931.8 4.0 while.10
  935.8 19.7 %custom-call.22 = f32[2,128,128]{1,2,0:T(8,128)S(1)} custom-call(f32[2,128,128]{2,1,0:T(8,128)S(1)} %get-tuple-element.32), custom_call_target="InvertDiagBlocksLowerTriangular" | custom-call | tf_op jit(solution)/shard_map/jit(_solve_triangular)/triangular_solve | solution.py:16
  957.2 1.9 fusion.83
  960.3 124.6 %all-reduce.13.cloned.1.call-done = f32[256,256]{0,1:T(8,128)} async-done(((f32[256,256]{0,1:T(8,128)}), f32[256,256]{0,1:T(8,128)}) %all-reduce.13.cloned.1.call-update) | async-done | bytes 262160 | tf_op jit(solution)/shard_map/psum | solution.py:83
  1087.0 11.7 %cholesky.316 = f32[128,128]{1,0:T(8,128)S(1)} custom-call(f32[128,128]{1,0:T(8,128)S(1)} %cholesky.355), custom_call_target="Cholesky" | custom-call | tf_op jit(solution)/shard_map/jit(cholesky)/cholesky | solution.py:15
  1098.8 9.8 custom-call.23
  1109.1 11.9 %cholesky.333 = f32[128,128]{1,0:T(8,128)S(1)} custom-call(f32[128,128]{1,0:T(8,128)S(1)} %convolution_subtract_fusion.4), custom_call_target="Cholesky" | custom-call | tf_op jit(solution)/shard_map/jit(cholesky)/cholesky | solution.py:15
  1123.8 4.1 while.11
  1127.9 19.7 %custom-call.24 = f32[2,128,128]{1,2,0:T(8,128)S(1)} custom-call(f32[2,128,128]{2,1,0:T(8,128)S(1)} %get-tuple-element.33), custom_call_target="InvertDiagBlocksLowerTriangular" | custom-call | tf_op jit(solution)/shard_map/jit(_solve_triangular)/triangular_solve | solution.py:16
  (127 shorter events, 50.9 us)
Async XLA Ops:
  7.2 29.4 %copy-start.3 = (s32[120]{0:T(128)S(1)}, s32[120]{0:T(128)}, u32[]{:S(2)}) copy-start(s32[120]{0:T(128)} %param.10) | copy-start | bytes 1444
  7.2 68.7 %all-gather.3.cloned.1.call-start = ((), (), s32[]{:S(2)}) async-start(), calls=%async_computation | async-start | bytes 5898240 | tf_op jit(solution)/shard_map/all_gather | solution.py:50
  36.5 357.1 %all-reduce.11.cloned.1.call-start = ((), (), s32[]{:S(2)}) async-start(), calls=%async_computation.1 | async-start | bytes 524288 | tf_op jit(solution)/shard_map/psum | solution.py:65
  108.2 15.7 %copy-start.2 = (s32[120]{0:T(128)S(1)}, s32[120]{0:T(128)}, u32[]{:S(2)}) copy-start(s32[120]{0:T(128)} %param.9) | copy-start | bytes 1444
  212.9 49.5 %copy-start = (f32[640,256]{1,0:T(8,128)S(1)}, f32[640,256]{1,0:T(8,128)}, u32[]{:S(2)}) copy-start(f32[640,256]{1,0:T(8,128)} %param.12) | copy-start | bytes 1966084
  212.9 26.2 %collective-permute-start = (f32[8,32768]{1,0:T(8,128)}, f32[8,32768]{1,0:T(8,128)S(1)}, u32[]{:S(2)}, u32[]{:S(2)}) collective-permute-start(f32[8,32768]{1,0:T(8,128)} %fusion), channel_id=1, source_target_pairs={{0,8},{8,16},{16,24},{1,9},{9,17},{17,25},{2,10},{10,18},{18,26},{... | collective-permute-start | bytes 3145736
  215.7 23.4 %collective-permute-start.1 = (f32[1,32768]{1,0:T(1,128)S(1)}, f32[1,32768]{1,0:T(1,128)S(1)}, u32[]{:S(2)}, u32[]{:S(2)}) collective-permute-start(f32[1,32768]{1,0:T(1,128)S(1)} %slice.54), channel_id=1, source_target_pairs={{0,16},{8,24},{1,17},{9,25},{2,18},{10,26},{3,19},{11,27},{4,20},{... | collective-permute-start | bytes 393224
  264.6 244.7 %all-gather.5.cloned.1.call-start = ((), (), s32[]{:S(2)}) async-start(), calls=%async_computation.2 | async-start | bytes 5898240 | tf_op jit(solution)/shard_map/all_gather | solution.py:50
  469.1 361.0 %all-reduce.15.cloned.1.call-start = ((), (), s32[]{:S(2)}) async-start(), calls=%async_computation.4 | async-start | bytes 1048576 | tf_op jit(solution)/shard_map/psum | solution.py:68
  647.4 25.9 %collective-permute-start.2 = (f32[8,32768]{1,0:T(8,128)S(1)}, f32[8,32768]{1,0:T(8,128)}, u32[]{:S(2)}, u32[]{:S(2)}) collective-permute-start(f32[8,32768]{1,0:T(8,128)S(1)} %fusion.1), channel_id=1, source_target_pairs={{0,8},{8,16},{16,24},{1,9},{9,17},{17,25},{2,10},{10,18},{18,26},{... | collective-permute-start | bytes 3145736
  649.8 23.5 %collective-permute-start.3 = (f32[1,32768]{1,0:T(1,128)S(1)}, f32[1,32768]{1,0:T(1,128)S(1)}, u32[]{:S(2)}, u32[]{:S(2)}) collective-permute-start(f32[1,32768]{1,0:T(1,128)S(1)} %slice.55), channel_id=1, source_target_pairs={{0,16},{8,24},{1,17},{9,25},{2,18},{10,26},{3,19},{11,27},{4,20},{... | collective-permute-start | bytes 393224
  698.7 386.2 %all-reduce.13.cloned.1.call-start = ((), (), s32[]{:S(2)}) async-start(), calls=%async_computation.3 | async-start | bytes 524288 | tf_op jit(solution)/shard_map/psum | solution.py:83
  830.1 64.1 %copy-start.1 = (f32[256,256]{1,0:T(8,128)S(1)}, f32[256,256]{1,0:T(8,128)}, u32[]{:S(2)}) copy-start(f32[256,256]{1,0:T(8,128)} %get-tuple-element.67) | copy-start | bytes 786436
Sparse Core Ops, SparseCore 0:
  36.7 39.1 all-gather.2
  264.7 128.9 all-reduce.10
  469.2 40.0 all-gather.4
  698.9 131.1 all-reduce.14
  959.2 125.6 all-reduce.12
where the time goes:
time: 1170 us; the launch traced here: 1160 us
  waiting for transfers between devices  504 us (43%)
  other arithmetic  227 us (19%)
  blocking collectives  177 us (15%)
  local copies, waits for them, and re-layouts  125 us (11%)
  matrix products  82.1 us (7%)
  between operations  22.1 us (2%)
    unnamed x3, blocking collectives  177 us
    another operation x27, other arithmetic, inverse_lower(): lower = jnp.linalg.cholesky(gram)  138 us
    psum x1, waiting for transfers between devices, body(): lax.psum((local_gram(raw_image), local_gram(pending)), ('col', 'row'))  131 us
    psum x1, waiting for transfers between devices, body(): inner_gram = lax.psum(local_gram(raw_image), ('col', 'row'))  129 us
    psum x1, waiting for transfers between devices, body(): final_gram = lax.psum(local_gram(pending), ('col', 'row'))  125 us
    unnamed x17, local copies, waits for them, and re-layouts  80.2 us
    all_gather x2, waiting for transfers between devices, body(): gathered = lax.all_gather(mapped_scaled, 'row', axis=0, tiled=True)  79.4 us
    another operation x9, other arithmetic, inverse_lower(): jax.scipy.linalg.solve_triangular(lower, jnp.eye(gram.shape[0], dtype=jnp...  79 us
  transfers between devices with their start and end apart: 9, of which 7 were waited for; matrix products, arithmetic and copies ran while one was open for 0% of the time, Pallas kernels for 0%

commit v1 on v0

--- a/solution.py
+++ b/solution.py
@@ -80,7 +80,7 @@
             )
         pending = apply_factor(image_block, inverse_lower(inner_gram))
         firsts.append(pending)
-    final_gram = lax.psum(local_gram(pending), ("col", "row"))
+    final_gram = jnp.sum(lax.all_gather(local_gram(pending), ("col", "row")), axis=0)
     basis = apply_factor(pending, inverse_lower(final_gram))
     total_images = rows_local * n_row * n_col
     root = jnp.sqrt(jnp.float32(total_images))

time: 1170 us -> 1120 us (0.957)
  waiting for transfers between devices: 504 us -> 455 us
    psum x1 -> x0, waiting for transfers between devices: 125 us -> none  [body(): final_gram = lax.psum(local_gram(pending), ('col', 'row'))]
    all_gather x0 -> x1, waiting for transfers between devices: none -> 75 us  [body(): lax.all_gather(local_gram(pending), ('col', 'row'))]
where the time goes in v1:
time: 1120 us; the launch traced here: 1110 us
  waiting for transfers between devices  455 us (41%)
  other arithmetic  230 us (21%)
  blocking collectives  177 us (16%)
  local copies, waits for them, and re-layouts  124 us (11%)
  matrix products  82.2 us (7%)
  between operations  22.1 us (2%)
    unnamed x3, blocking collectives  177 us
    another operation x27, other arithmetic, inverse_lower(): lower = jnp.linalg.cholesky(gram)  138 us
    psum x1, waiting for transfers between devices, body(): lax.psum((local_gram(raw_image), local_gram(pending)), ('col', 'row'))  131 us
    psum x1, waiting for transfers between devices, body(): inner_gram = lax.psum(local_gram(raw_image), ('col', 'row'))  129 us
    unnamed x17, local copies, waits for them, and re-layouts  80.2 us
    all_gather x2, waiting for transfers between devices, body(): gathered = lax.all_gather(mapped_scaled, 'row', axis=0, tiled=True)  79.4 us
    another operation x9, other arithmetic, inverse_lower(): jax.scipy.linalg.solve_triangular(lower, jnp.eye(gram.shape[0], dtype=jnp...  79 us
    all_gather x1, waiting for transfers between devices, body(): lax.all_gather(local_gram(pending), ('col', 'row'))  75 us
  transfers between devices with their start and end apart: 9, of which 7 were waited for; matrix products, arithmetic and copies ran while one was open for 0% of the time, Pallas kernels for 0%

profile of v1, /device:TPU:0, one launch (start us, length us, event | category | flops | bytes accessed | tf_op | source)
XLA Modules:
  0.0 1109.5 jit_solution(18070264037895639692)
XLA Ops:
  7.9 3.2 convert_reduce_fusion
  11.9 20.4 %all-reduce.1 = f32[20,128]{1,0:T(8,128)S(1)} all-reduce(f32[20,128]{1,0:T(8,128)S(1)} %fusion.55), channel_id=3, replica_groups=mesh['col'=4,'row'=8] {'col'}, use_global_device_ids=true, to_apply=%region_1.0.clone | all-reduce | flops 2560 | bytes 20480
  34.4 2.1 broadcast_multiply_fusion.1
  36.6 39.3 %all-gather.5.cloned.1.call-done = f32[5120,256]{1,0:T(8,128)} async-done(((f32[640,256]{1,0:T(8,128)}), f32[5120,256]{1,0:T(8,128)}) %all-gather.5.cloned.1.call-update) | async-done | bytes 5242896 | tf_op jit(solution)/shard_map/all_gather | solution.py:50
  75.9 12.1 %gather_fusion = f32[120,128,256]{2,1,0:T(8,128)} fusion(f32[40,128,256]{2,1,0:T(8,128)} %bitcast.167, s32[1024]{0:T(1024)S(1)} %pad_clamp_fusion), kind=kCustom, calls=%fused_computation | custom fusion | bytes 31457760 | tf_op jit(solution)/shard_map/gather | solution.py:52
  88.0 20.2 %convolution_bitcast_fusion.1 = f32[120,128,256]{1,2,0:T(8,128)} fusion(f32[120,128,256]{2,1,0:T(8,128)} %gather_fusion, bf16[120,128,128]{2,1,0:T(8,128)(2,1)} %param.8), kind=kOutput, calls=%fused_computation.11 | convolution fusion | flops 6039797760 | bytes 35389440 | tf_op jit(solution)/shard_map/sij,sjk->sik/dot_general | solution.py:53
  108.2 15.7 %copy.37 = f32[15,8,128,256]{3,1,2,0:T(8,128)} copy(f32[15,8,128,256]{2,3,1,0:T(8,128)} %bitcast.164) | data formatting | bytes 31457280
  123.9 10.5 fusion.53
  134.4 78.5 %fusion = f32[8,32768]{1,0:T(8,128)} fusion(f32[20,32768]{1,0:T(8,128)S(1)} %fusion.53), kind=kCustom, calls=%all-reduce-scatter | all-reduce-scatter fusion | flops 1048577 | bytes 3670528
  215.7 2.6 collective-permute-start.1
  219.0 20.1 %collective-permute-done.1 = f32[1,32768]{1,0:T(1,128)S(1)} collective-permute-done((f32[1,32768]{1,0:T(1,128)S(1)}, f32[1,32768]{1,0:T(1,128)S(1)}, u32[]{:S(2)}, u32[]{:S(2)}) %collective-permute-start.1) | collective-permute-done | bytes 131104
  239.1 21.2 %concatenate.3 = f32[17,32768]{1,0:T(8,128)} concatenate(f32[1,32768]{1,0:T(1,128)S(1)} %collective-permute-done.1, f32[8,32768]{1,0:T(8,128)S(1)} %collective-permute-done, f32[8,32768]{1,0:T(8,128)} %fusion), dimensions={0} | concatenate | bytes 4456448
  262.4 2.2 fusion.29
  264.6 129.0 %all-reduce.10.cloned.1.call-done = f32[256,256]{0,1:T(8,128)} async-done(((f32[256,256]{0,1:T(8,128)}), f32[256,256]{0,1:T(8,128)}) %all-reduce.10.cloned.1.call-update) | async-done | bytes 262160 | tf_op jit(solution)/shard_map/psum | solution.py:65
  395.7 11.7 %cholesky.214 = f32[128,128]{1,0:T(8,128)S(1)} custom-call(f32[128,128]{1,0:T(8,128)S(1)} %cholesky.346), custom_call_target="Cholesky" | custom-call | tf_op jit(solution)/shard_map/jit(cholesky)/cholesky | solution.py:15
  407.5 9.8 custom-call.17
  417.8 11.7 %cholesky.231 = f32[128,128]{1,0:T(8,128)S(1)} custom-call(f32[128,128]{1,0:T(8,128)S(1)} %convolution_subtract_fusion.7), custom_call_target="Cholesky" | custom-call | tf_op jit(solution)/shard_map/jit(cholesky)/cholesky | solution.py:15
  431.8 15.1 %while.8 = (s32[]{:T(128)}, f32[256,256]{1,0:T(8,128)S(1)}, s32[2,2]{1,0:T(2,128)S(1)}, f32[2,128,128]{2,1,0:T(8,128)S(1)}, s32[]{:T(128)}) while((s32[]{:T(128)}, f32[256,256]{1,0:T(8,128)S(1)}, s32[2,2]{1,0:T(2,128)S(1)}, f32[2,128,128]{2,1,0:T(8,128)S(1)}, s32[]{:T(128)}) %tuple.83), condition=%wide.while_cond, body=%wide.while_body.sunk | while | flops 2 | bytes 131181 | solution.py:16
  446.9 19.7 %custom-call.18 = f32[2,128,128]{1,2,0:T(8,128)S(1)} custom-call(f32[2,128,128]{2,1,0:T(8,128)S(1)} %get-tuple-element.30), custom_call_target="InvertDiagBlocksLowerTriangular" | custom-call | tf_op jit(solution)/shard_map/jit(_solve_triangular)/triangular_solve | solution.py:16
  469.1 40.2 %all-gather.7.cloned.1.call-done = f32[5120,256]{1,0:T(8,128)} async-done(((f32[640,256]{1,0:T(8,128)}), f32[5120,256]{1,0:T(8,128)}) %all-gather.7.cloned.1.call-update) | async-done | bytes 5242896 | tf_op jit(solution)/shard_map/all_gather | solution.py:50
  509.3 12.1 %gather_fusion.1 = f32[120,128,256]{2,1,0:T(8,128)} fusion(f32[40,128,256]{2,1,0:T(8,128)} %bitcast.168, s32[1024]{0:T(1024)S(1)} %pad_clamp_fusion), kind=kCustom, calls=%fused_computation.1 | custom fusion | bytes 31457760 | tf_op jit(solution)/shard_map/gather | solution.py:52
  521.4 20.2 %convolution_bitcast_fusion = f32[120,128,256]{1,2,0:T(8,128)} fusion(f32[120,128,256]{2,1,0:T(8,128)} %gather_fusion.1, bf16[120,128,128]{2,1,0:T(8,128)(2,1)} %param.8), kind=kOutput, calls=%fused_computation.10 | convolution fusion | flops 6039797760 | bytes 35389440 | tf_op jit(solution)/shard_map/sij,sjk->sik/dot_general | solution.py:53
  541.6 15.7 %copy.38 = f32[15,8,128,256]{3,1,2,0:T(8,128)} copy(f32[15,8,128,256]{2,3,1,0:T(8,128)} %bitcast.166) | data formatting | bytes 31457280
  557.3 11.6 %fusion.51 = f32[20,32768]{1,0:T(8,128)} fusion(f32[120,32768]{1,0:T(8,128)} %bitcast.163, f32[120]{0:T(128)S(1)} %compare_convert_fusion, s32[120]{0:T(128)S(1)} %copy-done.2), kind=kOutput, calls=%fused_computation.109 | convolution fusion | flops 943723200 | bytes 18351040 | tf_op jit(solution)/shard_map/dot_general | solution.py:56
  568.9 78.6 %fusion.1 = f32[8,32768]{1,0:T(8,128)S(1)} fusion(f32[20,32768]{1,0:T(8,128)} %fusion.51), kind=kCustom, calls=%all-reduce-scatter.1 | all-reduce-scatter fusion | flops 1048577 | bytes 3670528
  647.4 2.3 collective-permute-start.2
  653.4 19.9 %collective-permute-done.3 = f32[1,32768]{1,0:T(1,128)S(1)} collective-permute-done((f32[1,32768]{1,0:T(1,128)S(1)}, f32[1,32768]{1,0:T(1,128)S(1)}, u32[]{:S(2)}, u32[]{:S(2)}) %collective-permute-start.3) | collective-permute-done | bytes 131104
  673.3 21.2 %concatenate.4 = f32[17,32768]{1,0:T(8,128)} concatenate(f32[1,32768]{1,0:T(1,128)S(1)} %collective-permute-done.3, f32[8,32768]{1,0:T(8,128)} %collective-permute-done.2, f32[8,32768]{1,0:T(8,128)S(1)} %fusion.1), dimensions={0} | concatenate | bytes 4456448
  696.6 2.1 fusion.30
  698.8 131.3 %all-reduce.12.cloned.1.call-done = (f32[256,256]{0,1:T(8,128)}, f32[256,256]{1,0:T(8,128)}) async-done(((f32[256,256]{0,1:T(8,128)}, f32[256,256]{1,0:T(8,128)}), (f32[256,256]{0,1:T(8,128)}, f32[256,256]{1,0:T(8,128)})) %all-reduce.12.cloned.1.call-update) | async-done | bytes 524304 | tf_op jit(solution)/shard_map/psum | solution.py:68
  832.2 11.7 %cholesky.248 = f32[128,128]{1,0:T(8,128)S(1)} custom-call(f32[128,128]{1,0:T(8,128)S(1)} %cholesky.349), custom_call_target="Cholesky" | custom-call | tf_op jit(solution)/shard_map/jit(cholesky)/cholesky | solution.py:15
  844.0 9.8 custom-call.19
  854.3 11.7 %cholesky.265 = f32[128,128]{1,0:T(8,128)S(1)} custom-call(f32[128,128]{1,0:T(8,128)S(1)} %convolution_subtract_fusion.6), custom_call_target="Cholesky" | custom-call | tf_op jit(solution)/shard_map/jit(cholesky)/cholesky | solution.py:15
  868.7 4.0 while.9
  872.7 19.8 %custom-call.20 = f32[2,128,128]{1,2,0:T(8,128)S(1)} custom-call(f32[2,128,128]{2,1,0:T(8,128)S(1)} %get-tuple-element.31), custom_call_target="InvertDiagBlocksLowerTriangular" | custom-call | tf_op jit(solution)/shard_map/jit(_solve_triangular)/triangular_solve | solution.py:16
  895.2 11.7 %cholesky.282 = f32[128,128]{1,0:T(8,128)S(1)} custom-call(f32[128,128]{1,0:T(8,128)S(1)} %cholesky.352), custom_call_target="Cholesky" | custom-call | tf_op jit(solution)/shard_map/jit(cholesky)/cholesky | solution.py:15
  907.0 9.8 custom-call.21
  917.3 11.9 %cholesky.299 = f32[128,128]{1,0:T(8,128)S(1)} custom-call(f32[128,128]{1,0:T(8,128)S(1)} %convolution_subtract_fusion.5), custom_call_target="Cholesky" | custom-call | tf_op jit(solution)/shard_map/jit(cholesky)/cholesky | solution.py:15
  931.8 4.0 while.10
  935.8 19.7 %custom-call.22 = f32[2,128,128]{1,2,0:T(8,128)S(1)} custom-call(f32[2,128,128]{2,1,0:T(8,128)S(1)} %get-tuple-element.32), custom_call_target="InvertDiagBlocksLowerTriangular" | custom-call | tf_op jit(solution)/shard_map/jit(_solve_triangular)/triangular_solve | solution.py:16
  957.2 1.9 fusion.83
  960.3 75.0 %all-gather.9.cloned.1.call-done = f32[8192,256]{1,0:T(8,128)} async-done(((f32[256,256]{1,0:T(8,128)}), f32[8192,256]{1,0:T(8,128)}) %all-gather.9.cloned.1.call-update) | async-done | bytes 8388624 | tf_op jit(solution)/shard_map/all_gather | solution.py:83
  1035.3 3.9 reduce_sum.19
  1039.4 11.7 %cholesky.316 = f32[128,128]{1,0:T(8,128)S(1)} custom-call(f32[128,128]{1,0:T(8,128)S(1)} %cholesky.355), custom_call_target="Cholesky" | custom-call | tf_op jit(solution)/shard_map/jit(cholesky)/cholesky | solution.py:15
  1051.2 9.8 custom-call.23
  1061.5 11.9 %cholesky.333 = f32[128,128]{1,0:T(8,128)S(1)} custom-call(f32[128,128]{1,0:T(8,128)S(1)} %convolution_subtract_fusion.4), custom_call_target="Cholesky" | custom-call | tf_op jit(solution)/shard_map/jit(cholesky)/cholesky | solution.py:15
  1076.2 4.1 while.11
  1080.4 19.7 %custom-call.24 = f32[2,128,128]{1,2,0:T(8,128)S(1)} custom-call(f32[2,128,128]{2,1,0:T(8,128)S(1)} %get-tuple-element.33), custom_call_target="InvertDiagBlocksLowerTriangular" | custom-call | tf_op jit(solution)/shard_map/jit(_solve_triangular)/triangular_solve | solution.py:16
  (128 shorter events, 50.9 us)
Async XLA Ops:
  7.2 29.4 %copy-start.3 = (s32[120]{0:T(128)S(1)}, s32[120]{0:T(128)}, u32[]{:S(2)}) copy-start(s32[120]{0:T(128)} %param.10) | copy-start | bytes 1444
  7.2 68.7 %all-gather.5.cloned.1.call-start = ((), (), s32[]{:S(2)}) async-start(), calls=%async_computation | async-start | bytes 5898240 | tf_op jit(solution)/shard_map/all_gather | solution.py:50
  36.5 357.1 %all-reduce.10.cloned.1.call-start = ((), (), s32[]{:S(2)}) async-start(), calls=%async_computation.1 | async-start | bytes 524288 | tf_op jit(solution)/shard_map/psum | solution.py:65
  108.2 15.7 %copy-start.2 = (s32[120]{0:T(128)S(1)}, s32[120]{0:T(128)}, u32[]{:S(2)}) copy-start(s32[120]{0:T(128)} %param.9) | copy-start | bytes 1444
  212.9 49.5 %copy-start = (f32[640,256]{1,0:T(8,128)S(1)}, f32[640,256]{1,0:T(8,128)}, u32[]{:S(2)}) copy-start(f32[640,256]{1,0:T(8,128)} %param.12) | copy-start | bytes 1966084
  212.9 26.2 %collective-permute-start = (f32[8,32768]{1,0:T(8,128)}, f32[8,32768]{1,0:T(8,128)S(1)}, u32[]{:S(2)}, u32[]{:S(2)}) collective-permute-start(f32[8,32768]{1,0:T(8,128)} %fusion), channel_id=1, source_target_pairs={{0,8},{8,16},{16,24},{1,9},{9,17},{17,25},{2,10},{10,18},{18,26},{... | collective-permute-start | bytes 3145736
  215.7 23.4 %collective-permute-start.1 = (f32[1,32768]{1,0:T(1,128)S(1)}, f32[1,32768]{1,0:T(1,128)S(1)}, u32[]{:S(2)}, u32[]{:S(2)}) collective-permute-start(f32[1,32768]{1,0:T(1,128)S(1)} %slice.54), channel_id=1, source_target_pairs={{0,16},{8,24},{1,17},{9,25},{2,18},{10,26},{3,19},{11,27},{4,20},{... | collective-permute-start | bytes 393224
  264.6 244.7 %all-gather.7.cloned.1.call-start = ((), (), s32[]{:S(2)}) async-start(), calls=%async_computation.2 | async-start | bytes 5898240 | tf_op jit(solution)/shard_map/all_gather | solution.py:50
  469.1 361.0 %all-reduce.12.cloned.1.call-start = ((), (), s32[]{:S(2)}) async-start(), calls=%async_computation.4 | async-start | bytes 1048576 | tf_op jit(solution)/shard_map/psum | solution.py:68
  647.4 25.9 %collective-permute-start.2 = (f32[8,32768]{1,0:T(8,128)S(1)}, f32[8,32768]{1,0:T(8,128)}, u32[]{:S(2)}, u32[]{:S(2)}) collective-permute-start(f32[8,32768]{1,0:T(8,128)S(1)} %fusion.1), channel_id=1, source_target_pairs={{0,8},{8,16},{16,24},{1,9},{9,17},{17,25},{2,10},{10,18},{18,26},{... | collective-permute-start | bytes 3145736
  649.8 23.5 %collective-permute-start.3 = (f32[1,32768]{1,0:T(1,128)S(1)}, f32[1,32768]{1,0:T(1,128)S(1)}, u32[]{:S(2)}, u32[]{:S(2)}) collective-permute-start(f32[1,32768]{1,0:T(1,128)S(1)} %slice.55), channel_id=1, source_target_pairs={{0,16},{8,24},{1,17},{9,25},{2,18},{10,26},{3,19},{11,27},{4,20},{... | collective-permute-start | bytes 393224
  698.7 336.6 %all-gather.9.cloned.1.call-start = ((), (), s32[]{:S(2)}) async-start(), calls=%async_computation.3 | async-start | bytes 8650752 | tf_op jit(solution)/shard_map/all_gather | solution.py:83
  830.1 64.1 %copy-start.1 = (f32[256,256]{1,0:T(8,128)S(1)}, f32[256,256]{1,0:T(8,128)}, u32[]{:S(2)}) copy-start(f32[256,256]{1,0:T(8,128)} %get-tuple-element.67) | copy-start | bytes 786436
Sparse Core Ops, SparseCore 0:
  36.7 39.1 all-gather.4
  264.7 128.9 all-reduce.9
  469.2 40.0 all-gather.6
  698.9 131.1 all-reduce.11
  959.3 76.0 all-gather.8
